TPU v7x, 512 devices: a whole 4x8x8 slice. The times are simulated.
512 devices in a mesh: dp: 16 (over y, core), seq: 32 (over z, x).
Axes of the slice: x: 4, y: 8, z: 8, core: 2. Of those that a mesh axis runs over, the one named last changes fastest.
Arguments:
- hidden: bfloat16 [65536, 2048], P(('dp', 'seq')), may hold values from -6 to 6
- queries: bfloat16 [65536, 2048], P(('dp', 'seq')), may hold values from -360 to 360
- values: bfloat16 [65536, 512], P(('dp', 'seq')), may hold values from -6 to 6
- row_target: int32 [65536], P(('dp', 'seq')), may hold values from 0 to 4095, as said below
- key_weight: bfloat16 [2048, 512], P(('dp', 'seq')), may hold values from -0.125 to 0.125
- dialogue_lengths: int32 [16, 64], P('dp'), may hold values from 1 to 256, 4096 in all within a row
- teacher_pick: int32 [65536, 128], P(('dp', 'seq')), may hold values from 0 to 65279
- teacher_prob: float32 [65536, 128], P(('dp', 'seq')), may hold values from 0.02 to 1
Outputs:
- attn_out: bfloat16 [65536, 2048], P(('dp', 'seq'))
- token_loss: float32 [65536], P(('dp', 'seq'))
- weight_grad: float32 [2048, 512], P(('dp', 'seq'))
Inputs may be any that keep to these rules, and one draw needn't show every extreme that they name: Within each pack, row_target holds every position 0 to 4095 once. Of the 128 rows of one device, at most 6 have targets in one block of 128 positions (target // 128 names the block), and in every draw some device sends exactly 6 to some block.
All inputs are finite; a program needn't handle non-finite values.
Results may differ from a plain program's by a relative error of at most 0.012.
The roundings to bfloat16 on the way count: a program that leaves them out, or rounds other values in their place, can miss the bound.
Values may be sent and summed in bfloat16 or wider, within the bound.
No kernel may reach another device: no remote copies, remote signals or barrier semaphores. Data moves between devices by JAX's collectives and lax.ppermute only.
A program may use at most 64 MiB of HBM per device.

v0:
```python
import jax
import jax.numpy as jnp
from jax import lax
from jax.sharding import PartitionSpec as P

HEAD_DIM = 128
SPAN = 2
negative = -1e30
rope_base = 500000.0


def side_by_side(arrays, axis, split_dim, concat_dim, along):
    ends, at = ([], 0)
    for a in arrays[:-1]:
        at += a.shape[along]
        ends.append(at)
    both = jnp.concatenate(arrays, axis=along)
    return tuple(
        jnp.split(
            lax.all_to_all(both, axis, split_axis=split_dim, concat_axis=concat_dim, tiled=True),
            ends,
            axis=along,
        )
    )


def shifted(shard, axis, by):
    devices = lax.axis_size(axis)
    pairs = [(i, i + by) for i in range(devices) if 0 <= i + by < devices]
    return lax.ppermute(shard, axis, pairs)


def rotate(matrix, positions, direction):
    count = matrix.shape[0]
    split = matrix.reshape(count, -1, HEAD_DIM)
    halfway = HEAD_DIM // 2
    frequency = rope_base ** (-2.0 * jnp.arange(halfway, dtype=jnp.float32) / HEAD_DIM)
    angle = positions.astype(jnp.float32)[:, None] * frequency[None, :]
    cosine = jnp.cos(angle)[:, None, :]
    sine = direction * jnp.sin(angle)[:, None, :]
    first_half = split[..., :halfway]
    second_half = split[..., halfway:]
    joined = jnp.concatenate(
        [first_half * cosine - second_half * sine, second_half * cosine + first_half * sine],
        axis=-1,
    )
    return joined.reshape(count, -1)


def dialogue_starts(lengths, positions):
    ending = jnp.cumsum(lengths)
    picked = jnp.where(ending[None, :] <= positions[:, None], lengths[None, :], 0)
    return jnp.sum(picked, axis=1)


def block_targets(label_index, label_prob, key_start, width):
    within = label_index - key_start
    columns = jnp.arange(width, dtype=jnp.int32)
    matches = within[..., None] == columns[None, None, None, :]
    table = jnp.sum(jnp.where(matches, label_prob[..., None], 0.0), axis=2)
    return jnp.transpose(table, (1, 0, 2))


def project_keys(inputs, key_weight):
    return jnp.dot(
        inputs,
        lax.all_gather(key_weight, ("dp", "seq"), axis=0, tiled=True),
        preferred_element_type=jnp.float32,
    )


def move_rows(first_rows, second_rows, third_rows, row_places):
    return (
        *side_by_side((first_rows, second_rows, third_rows), "seq", 0, 0, 1),
        lax.all_to_all(row_places, "seq", split_axis=0, concat_axis=0, tiled=True),
    )


def guarded(compute, operands):
    return compute(*operands)


def local(
    hidden, queries, values, row_target, key_weight, dialogue_lengths, teacher_pick, teacher_prob
):
    local_rows = hidden.shape[0]
    seq_count = lax.axis_size("seq")
    seq_index = lax.axis_index("seq")
    device_count = seq_count * lax.axis_size("dp")
    capacity = local_rows // seq_count + local_rows // (2 * seq_count)
    head_count = queries.shape[1] // HEAD_DIM
    kv_count = values.shape[1] // HEAD_DIM
    group_size = head_count // kv_count
    top_count = teacher_pick.shape[1] // head_count
    scaling = HEAD_DIM ** (-0.5)
    destination = row_target // local_rows
    offset_in = row_target - destination * local_rows
    one_hot = (destination[:, None] == jnp.arange(seq_count, dtype=jnp.int32)[None, :]).astype(
        jnp.int32
    )
    rank_in = jnp.sum((jnp.cumsum(one_hot, axis=0) - one_hot) * one_hot, axis=1)
    slot_of = destination * capacity + rank_in

    def parcel(data, filler):
        holder = jnp.full((seq_count * capacity,) + data.shape[1:], filler, data.dtype)
        return holder.at[slot_of].set(data)

    def settle(data, places):
        holder = jnp.zeros((local_rows,) + data.shape[1:], data.dtype)
        return holder.at[places].set(data, mode="drop")

    positions = seq_index * local_rows + jnp.arange(local_rows, dtype=jnp.int32)
    received = move_rows(
        parcel(hidden, 0), parcel(queries, 0), parcel(values, 0), parcel(offset_in, local_rows)
    )
    hidden_seq = settle(received[0], received[3])
    queries_seq = settle(received[1], received[3])
    values_seq = settle(received[2], received[3])
    keys_seq = rotate(project_keys(hidden_seq, key_weight), positions, 1.0).astype(jnp.bfloat16)
    starts = dialogue_starts(dialogue_lengths[0], positions)
    reach = (positions - starts + 1)[:, None]
    label_index = (starts[:, None] + teacher_pick % reach).reshape(
        local_rows, head_count, top_count
    )
    label_prob = teacher_prob.reshape(local_rows, head_count, top_count)
    target_mass = jnp.sum(label_prob, axis=2).T.reshape(kv_count, group_size, local_rows)
    entropy = jnp.sum(label_prob * jnp.log(label_prob), axis=(1, 2))
    query_heads = queries_seq.reshape(local_rows, kv_count, group_size, HEAD_DIM)
    earliest = jnp.min(starts)
    blocks = [(keys_seq, values_seq)]
    for distance in range(1, SPAN + 1):
        blocks.append(shifted((keys_seq, values_seq), "seq", distance))

    def scores_of(key_block, key_start):
        key_heads = key_block.reshape(local_rows, kv_count, HEAD_DIM)
        score = (
            jnp.einsum("tkgd,wkd->kgtw", query_heads, key_heads, preferred_element_type=jnp.float32)
            * scaling
        )
        key_pos = key_start + jnp.arange(local_rows, dtype=jnp.int32)
        allowed = (key_pos[None, :] >= starts[:, None]) & (key_pos[None, :] <= positions[:, None])
        held = jnp.where(allowed[None, None], score, negative)
        table = block_targets(label_index, label_prob, key_start, local_rows)
        return (score, held, table.reshape(kv_count, group_size, local_rows, local_rows))

    def first_pass(key_block, key_start):
        score, held, table = scores_of(key_block, key_start)
        block_top = jnp.max(held, axis=-1)
        block_total = jnp.sum(jnp.exp(held - block_top[..., None]), axis=-1)
        return (block_top, block_total, jnp.sum(table * score, axis=-1))

    tops, totals, pickings, alive_list = ([], [], [], [])
    for distance, (key_block, value_block) in enumerate(blocks):
        key_start = (seq_index - distance) * local_rows
        alive = earliest < key_start + local_rows
        alive_list.append((alive, key_start))
        block_top, block_total, picking = guarded(first_pass, (key_block, key_start))
        tops.append(block_top)
        totals.append(block_total)
        pickings.append(picking)
    top_all = jnp.max(jnp.stack(tops), axis=0)
    total_all = jnp.sum(jnp.stack(totals) * jnp.exp(jnp.stack(tops) - top_all[None]), axis=0)
    lse = top_all + jnp.log(total_all)
    picked_all = jnp.sum(jnp.stack(pickings), axis=0)
    token_loss = (
        entropy - jnp.sum(picked_all, axis=(0, 1)) + jnp.sum(target_mass * lse, axis=(0, 1))
    ) / head_count

    def second_pass(key_block, value_block, key_start):
        score, held, table = scores_of(key_block, key_start)
        weight = jnp.exp(held - lse[..., None])
        value_heads = value_block.reshape(local_rows, kv_count, HEAD_DIM)
        partial_value = jnp.einsum(
            "kgtw,wkd->tkgd",
            weight.astype(jnp.bfloat16),
            value_heads,
            preferred_element_type=jnp.float32,
        )
        slope = ((weight * target_mass[..., None] - table) / head_count).astype(jnp.bfloat16)
        gradient = (
            jnp.einsum("kgtw,tkgd->wkd", slope, query_heads, preferred_element_type=jnp.float32)
            * scaling
        )
        return (partial_value, gradient.reshape(local_rows, kv_count * HEAD_DIM))

    output_sum = jnp.zeros((local_rows, kv_count, group_size, HEAD_DIM), jnp.float32)
    block_grads = []
    for distance, (key_block, value_block) in enumerate(blocks):
        alive, key_start = alive_list[distance]
        partial_value, gradient = guarded(second_pass, (key_block, value_block, key_start))
        output_sum = output_sum + partial_value
        block_grads.append(gradient)
    attn_out = output_sum.astype(jnp.bfloat16).reshape(local_rows, head_count * HEAD_DIM)
    rotated_grad = block_grads[0]
    for distance in range(1, SPAN + 1):
        rotated_grad = rotated_grad + shifted(
            block_grads[distance].astype(jnp.bfloat16), "seq", -distance
        ).astype(jnp.float32)
    key_grad = rotate(rotated_grad, positions, -1.0).astype(jnp.bfloat16)
    inverse_root = (local_rows * device_count) ** (-0.5)
    weight_grad = lax.psum_scatter(
        jnp.einsum("td,tc->dc", hidden_seq, key_grad, preferred_element_type=jnp.float32)
        * inverse_root,
        ("dp", "seq"),
        scatter_dimension=0,
        tiled=True,
    )
    return (attn_out, token_loss, weight_grad)


def solution(mesh):
    placed = (
        P(("dp", "seq"), None),
        P(("dp", "seq"), None),
        P(("dp", "seq"), None),
        P(("dp", "seq")),
        P(("dp", "seq"), None),
        P("dp", None),
        P(("dp", "seq"), None),
        P(("dp", "seq"), None),
    )
    return jax.shard_map(
        local,
        mesh=mesh,
        in_specs=placed,
        out_specs=(P(("dp", "seq"), None), P(("dp", "seq")), P(("dp", "seq"), None)),
        check_vma=False,
    )
```

profile of v0, /device:TPU:24, one launch (start us, length us, event | category | flops | bytes accessed | tf_op | source)
XLA Modules:
  0.0 468.3 jit_solution(1909932500916336995)
XLA Ops:
  10.7 13.2 %all-to-all-start = ((s32[32,6,1]{1,2,0:T(1,128)}), s32[32,6,1]{1,2,0:T(1,128)S(1)}, u32[]{:S(2)}, u32[]{:S(2)}) async-start(s32[32,6,1]{1,2,0:T(1,128)} %bitcast), calls=%async_computation | async-start | bytes 32768 | tf_op jit(solution)/shard_map/all_to_all | solution.py:75
  23.9 1.5 scatter_custom_fusion.3
  25.4 2.1 scatter_custom_fusion.2
  27.5 2.1 scatter_custom_fusion.1
  29.8 1.7 all_to_all.19
  31.5 2.1 all-to-all-done
  33.6 7.8 %all-to-all-start.1 = ((bf16[32,6,4608]{2,1,0:T(8,128)(2,1)}), bf16[32,6,4608]{2,1,0:T(8,128)(2,1)S(1)}, u32[]{:S(2)}, u32[]{:S(2)}) async-start(bf16[32,6,4608]{2,1,0:T(8,128)(2,1)} %all_to_all.19), calls=%async_computation.1 | async-start | bytes 4718592 | tf_op jit(solution)/shard_map/all_to_all | solution.py:20
  44.4 1.4 copy.109
  45.8 2.2 copy.113
  48.1 2.2 copy.107
  50.3 13.4 %select_reduce_fusion.1 = (f32[128,16,128]{2,1,0:T(8,128)}, f32[128,16,128]{2,1,0:T(8,128)}, f32[128,16,128]{2,1,0:T(8,128)}) fusion(s32[128,16,8]{2,1,0:T(8,128)S(1)} %copy.111, f32[128,16,8]{2,1,0:T(8,128)} %copy.109, s32[128,16,8]{2,1,0:T(8,128)} %copy.113, s32[128,16,8]{2,1,0:T(8,128)} %copy.107), kind=kLoop, calls=%fused_computation.9 | loop fusion | flops 18087936 | bytes 3407872 | tf_op jit(solution)/shard_map/reduce_sum | solution.py:60
  63.6 2.6 copy.114
  66.3 2.6 copy.112
  68.8 1.4 copy.110
  72.8 25.2 %all-to-all-done.1 = bf16[32,6,4608]{2,1,0:T(8,128)(2,1)S(1)} async-done(((bf16[32,6,4608]{2,1,0:T(8,128)(2,1)}), bf16[32,6,4608]{2,1,0:T(8,128)(2,1)S(1)}, u32[]{:S(2)}, u32[]{:S(2)}) %all-to-all-start.1) | async-done | bytes 1769504 | tf_op jit(solution)/shard_map/all_to_all | solution.py:20
  98.0 1.6 all_to_all.21
  99.6 2.6 scatter_custom_fusion.6
  102.2 2.4 scatter_custom_fusion.5
  104.9 31.5 %all-gather.3.cloned.1.call-done = bf16[512,4,512]{2,1,0:T(4,128)(2,1)} async-done(((bf16[1,4,512]{2,1,0:T(4,128)(2,1)}), bf16[512,4,512]{2,1,0:T(4,128)(2,1)}) %all-gather.3.cloned.1.call-update) | async-done | bytes 2097168 | tf_op jit(solution)/shard_map/all_gather | solution.py:67
  136.5 4.0 reshape.528
  140.4 2.1 fusion.77
  143.2 4.5 collective-permute-start.1
  147.7 2.7 collective-permute-start
  151.7 2.0 collective-permute-done
  159.4 6.5 %collective-permute-done.5 = bf16[128,512]{0,1:T(8,128)(2,1)S(1)} collective-permute-done((bf16[128,512]{0,1:T(8,128)(2,1)S(1)}, bf16[128,512]{0,1:T(8,128)(2,1)S(1)}, u32[]{:S(2)}, u32[]{:S(2)}) %collective-permute-start.5) | collective-permute-done | bytes 131104 | tf_op jit(solution)/shard_map/ppermute | solution.py:30
  165.9 2.1 collective-permute-done.4
  168.7 2.7 convolution_multiply_fusion
  171.4 1.8 scatter_custom_fusion.4
  173.2 4.5 collective-permute-start.2
  177.7 6.0 %collective-permute-start.3 = (bf16[128,512]{1,0:T(8,128)(2,1)S(1)}, bf16[128,512]{1,0:T(8,128)(2,1)}, u32[]{:S(2)}, u32[]{:S(2)}) collective-permute-start(bf16[128,512]{1,0:T(8,128)(2,1)S(1)} %scatter_custom_fusion.4), channel_id=1, source_target_pairs={{0,2},{1,3},{2,4},{3,5},{4,6},{5,7},{6,8},{7,9},{8,10},{9,11},{10,... | collective-permute-start | bytes 393224 | tf_op jit(solution)/shard_map/ppermute | solution.py:30
  184.4 1.7 copy.102
  190.7 269.5 %all-reduce.3.cloned.1.call-done = f32[2048,512]{1,0:T(8,128)} async-done(((f32[2048,512]{1,0:T(8,128)}), f32[2048,512]{1,0:T(8,128)}) %all-reduce.3.cloned.1.call-update) | async-done | bytes 4194320
  (108 shorter events, 24.1 us)
Async XLA Ops:
  7.2 129.3 %all-gather.3.cloned.1.call-start = ((), (), s32[]{:S(2)}) async-start(), calls=%async_computation.2 | async-start | bytes 2101248 | tf_op jit(solution)/shard_map/all_gather | solution.py:67
  10.7 22.9 %all-to-all-start = ((s32[32,6,1]{1,2,0:T(1,128)}), s32[32,6,1]{1,2,0:T(1,128)S(1)}, u32[]{:S(2)}, u32[]{:S(2)}) async-start(s32[32,6,1]{1,2,0:T(1,128)} %bitcast), calls=%async_computation | async-start | bytes 32768 | tf_op jit(solution)/shard_map/all_to_all | solution.py:75
  29.7 12.2 %copy-start.15 = (s32[1,64]{1,0:T(1,128)S(1)}, s32[1,64]{1,0:T(1,128)}, u32[]{:S(2)}) copy-start(s32[1,64]{1,0:T(1,128)} %param.13) | copy-start | bytes 772
  29.8 12.5 %copy-start.9 = (s32[128,128]{1,0:T(8,128)S(1)}, s32[128,128]{1,0:T(8,128)}, u32[]{:S(2)}) copy-start(s32[128,128]{1,0:T(8,128)} %param.14) | copy-start | bytes 196612
  31.5 12.8 %copy-start.7 = (f32[128,128]{1,0:T(8,128)S(1)}, f32[128,128]{1,0:T(8,128)}, u32[]{:S(2)}) copy-start(f32[128,128]{1,0:T(8,128)} %param.15) | copy-start | bytes 196612
  33.6 64.4 %all-to-all-start.1 = ((bf16[32,6,4608]{2,1,0:T(8,128)(2,1)}), bf16[32,6,4608]{2,1,0:T(8,128)(2,1)S(1)}, u32[]{:S(2)}, u32[]{:S(2)}) async-start(bf16[32,6,4608]{2,1,0:T(8,128)(2,1)} %all_to_all.19), calls=%async_computation.1 | async-start | bytes 4718592 | tf_op jit(solution)/shard_map/all_to_all | solution.py:20
  41.4 418.7 %all-reduce.3.cloned.1.call-start = ((), (), s32[]{:S(2)}) async-start(), calls=%async_computation.3 | async-start | bytes 8388608
  42.0 1.9 copy-start.13
  42.5 1.3 copy-start.11
  63.6 5.2 %copy-start.6 = (f32[128,16,128]{2,1,0:T(8,128)S(1)}, f32[128,16,128]{2,1,0:T(8,128)}, u32[]{:S(2)}) copy-start(f32[128,16,128]{2,1,0:T(8,128)} %get-tuple-element.19) | copy-start | bytes 3145732
  63.6 6.7 %copy-start.12 = (s32[128]{0:T(128)S(1)}, s32[128]{0:T(128)}, u32[]{:S(2)}) copy-start(s32[128]{0:T(128)} %copy-done.11) | copy-start | bytes 1540
  63.6 6.7 %copy-start.14 = (s32[128]{0:T(128)S(1)}, s32[128]{0:T(128)}, u32[]{:S(2)}) copy-start(s32[128]{0:T(128)} %copy-done.13) | copy-start | bytes 1540
  72.8 32.2 %copy-start.17 = (s32[192,1]{0,1:T(1,128)}, s32[192,1]{0,1:T(1,128)S(1)}, u32[]{:S(2)}) copy-start(s32[192,1]{0,1:T(1,128)S(1)} %compare_select_fusion) | copy-start | bytes 2308
  140.4 10.3 %copy-start.4 = (f32[16,128,128]{1,2,0:T(8,128)S(1)}, f32[16,128,128]{1,2,0:T(8,128)}, u32[]{:S(2)}) copy-start(f32[16,128,128]{1,2,0:T(8,128)} %copy.110) | copy-start | bytes 3145732
  143.2 8.1 %collective-permute-start.1 = (bf16[128,512]{0,1:T(8,128)(2,1)S(1)}, bf16[128,512]{0,1:T(8,128)(2,1)S(1)}, u32[]{:S(2)}, u32[]{:S(2)}) collective-permute-start(bf16[128,512]{0,1:T(8,128)(2,1)S(1)} %bitcast.171), channel_id=1, source_target_pairs={{0,2},{1,3},{2,4},{3,5},{4,6},{5,7},{6,8},{7,9},{8,10},{9,11},{10,... | collective-permute-start | bytes 393224 | tf_op jit(solution)/shard_map/ppermute | solution.py:30
  147.7 5.9 %collective-permute-start = (bf16[128,512]{0,1:T(8,128)(2,1)S(1)}, bf16[128,512]{0,1:T(8,128)(2,1)S(1)}, u32[]{:S(2)}, u32[]{:S(2)}) collective-permute-start(bf16[128,512]{0,1:T(8,128)(2,1)S(1)} %bitcast.172), channel_id=1, source_target_pairs={{0,1},{1,2},{2,3},{3,4},{4,5},{5,6},{6,7},{7,8},{8,9},{9,10},{10,1... | collective-permute-start | bytes 393224 | tf_op jit(solution)/shard_map/ppermute | solution.py:30
  150.4 3.6 copy-start.2
  150.7 8.2 %copy-start = (f32[4,4,128,128]{2,3,1,0:T(8,128)}, f32[4,4,128,128]{2,3,1,0:T(8,128)S(1)}, u32[]{:S(2)}) copy-start(f32[4,4,128,128]{2,3,1,0:T(8,128)S(1)} %get-tuple-element.48) | copy-start | bytes 3145732
  150.8 3.6 copy-start.3
  154.4 4.5 copy-start.5
  156.3 9.6 %collective-permute-start.5 = (bf16[128,512]{0,1:T(8,128)(2,1)S(1)}, bf16[128,512]{0,1:T(8,128)(2,1)S(1)}, u32[]{:S(2)}, u32[]{:S(2)}) collective-permute-start(bf16[128,512]{0,1:T(8,128)(2,1)S(1)} %bitcast.170), channel_id=1, source_target_pairs={{2,0},{3,1},{4,2},{5,3},{6,4},{7,5},{8,6},{9,7},{10,8},{11,9},{12,... | collective-permute-start | bytes 393224 | tf_op jit(solution)/shard_map/ppermute | solution.py:30
  157.6 10.4 %collective-permute-start.4 = (bf16[128,512]{0,1:T(8,128)(2,1)S(1)}, bf16[128,512]{0,1:T(8,128)(2,1)S(1)}, u32[]{:S(2)}, u32[]{:S(2)}) collective-permute-start(bf16[128,512]{0,1:T(8,128)(2,1)S(1)} %bitcast.169), channel_id=1, source_target_pairs={{1,0},{2,1},{3,2},{4,3},{5,4},{6,5},{7,6},{8,7},{9,8},{10,9},{11,1... | collective-permute-start | bytes 393224 | tf_op jit(solution)/shard_map/ppermute | solution.py:30
  168.6 15.0 %copy-start.8 = (f32[128,128]{1,0:T(8,128)S(1)}, f32[128,128]{1,0:T(8,128)}, u32[]{:S(2)}) copy-start(f32[128,128]{1,0:T(8,128)} %param.15) | copy-start | bytes 196612
  171.4 15.8 %copy-start.1 = (f32[4,4,128,128]{2,3,1,0:T(8,128)S(1)}, f32[4,4,128,128]{2,3,1,0:T(8,128)}, u32[]{:S(2)}) copy-start(f32[4,4,128,128]{2,3,1,0:T(8,128)} %copy-done) | copy-start | bytes 3145732
  173.2 11.2 %collective-permute-start.2 = (bf16[128,512]{1,0:T(8,128)(2,1)S(1)}, bf16[128,512]{1,0:T(8,128)(2,1)}, u32[]{:S(2)}, u32[]{:S(2)}) collective-permute-start(bf16[128,512]{1,0:T(8,128)(2,1)S(1)} %scatter_custom_fusion.4), channel_id=1, source_target_pairs={{0,1},{1,2},{2,3},{3,4},{4,5},{5,6},{6,7},{7,8},{8,9},{9,10},{10,1... | collective-permute-start | bytes 393224 | tf_op jit(solution)/shard_map/ppermute | solution.py:30
  177.7 8.4 %collective-permute-start.3 = (bf16[128,512]{1,0:T(8,128)(2,1)S(1)}, bf16[128,512]{1,0:T(8,128)(2,1)}, u32[]{:S(2)}, u32[]{:S(2)}) collective-permute-start(bf16[128,512]{1,0:T(8,128)(2,1)S(1)} %scatter_custom_fusion.4), channel_id=1, source_target_pairs={{0,2},{1,3},{2,4},{3,5},{4,6},{5,7},{6,8},{7,9},{8,10},{9,11},{10,... | collective-permute-start | bytes 393224 | tf_op jit(solution)/shard_map/ppermute | solution.py:30
  187.5 2.7 copy-start.10
  187.5 2.7 copy-start.16
Sparse Core Ops, SparseCore 0:
  12.2 124.2 all-gather.2
  171.5 288.5 all-reduce.2
where the time goes:
time: 469 us; the launch traced here: 468 us
  waiting for transfers between devices  340 us (72%)
  local copies, waits for them, and re-layouts  41.6 us (9%)
  starting transfers between devices  41.3 us (9%)
  other arithmetic  21.7 us (5%)
  between operations  14.6 us (3%)
  matrix products  9.27 us (2%)
    unnamed x3, waiting for transfers between devices  270 us
    all_gather x1, waiting for transfers between devices, project_keys(): lax.all_gather(key_weight, ('dp', 'seq'), axis=0, tiled=True)  31.5 us
    all_to_all x1, waiting for transfers between devices, side_by_side(): lax.all_to_all(both, axis, split_axis=split_dim, concat_axis=concat_dim,...  25.2 us
    ppermute x6, starting transfers between devices, shifted(): return lax.ppermute(shard, axis, pairs)  20.3 us
    reduce_sum x1, other arithmetic, block_targets(): table = jnp.sum(jnp.where(matches, label_prob[..., None], 0.0), axis=2)  13.4 us
    all_to_all x1, starting transfers between devices, move_rows(): lax.all_to_all(row_places, 'seq', split_axis=0, concat_axis=0, tiled=True)  13.2 us
    ppermute x6, waiting for transfers between devices, shifted(): return lax.ppermute(shard, axis, pairs)  10.8 us
  transfers between devices with their start and end apart: 10, of which 8 were waited for; matrix products, arithmetic and copies ran while one was open for 12% of the time, Pallas kernels for 0%

commit v1 on v0

--- a/solution.py
+++ b/solution.py
@@ -64,7 +64,12 @@
 def project_keys(inputs, key_weight):
     return jnp.dot(
         inputs,
-        lax.all_gather(key_weight, ("dp", "seq"), axis=0, tiled=True),
+        jnp.concatenate(
+            lax.all_to_all(
+                jnp.stack([key_weight] * lax.axis_size(("dp", "seq"))), ("dp", "seq"), 0, 0
+            ),
+            axis=0,
+        ),
         preferred_element_type=jnp.float32,
     )
 

time: 469 us -> 496 us (1.058)
  blocking collectives: 0 us -> 65 us
  waiting for transfers between devices: 340 us -> 292 us
  starting transfers between devices: 41.3 us -> 46.9 us
    all_to_all x0 -> x1, blocking collectives: none -> 65 us  [side_by_side(): lax.all_to_all(both, axis, split_axis=split_dim, concat_axis=concat_dim,...]
    all_gather x1 -> x0, waiting for transfers between devices: 31.5 us -> none  [project_keys(): lax.all_gather(key_weight, ('dp', 'seq'), axis=0, tiled=True)]
    all_to_all x1, waiting for transfers between devices: 25.2 us -> 11.9 us  [project_keys(): lax.all_to_all(jnp.stack([key_weight] * lax.axis_size(('dp', 'seq'))), ('...]
    all_to_all x1, starting transfers between devices: 7.84 us -> 13.8 us  [project_keys(): lax.all_to_all(jnp.stack([key_weight] * lax.axis_size(('dp', 'seq'))), ('...]
    unnamed x3 -> x2, waiting for transfers between devices: 270 us -> 268 us
  transfers between devices with their start and end apart: 10 -> 9, of which waited for: 8 -> 7; matrix products, arithmetic and copies ran while one was open for 12% -> 11% of each run, Pallas kernels for 0% -> 0%
where the time goes in v1:
time: 496 us; the launch traced here: 495 us
  waiting for transfers between devices  292 us (59%)
  blocking collectives  65 us (13%)
  starting transfers between devices  46.9 us (9%)
  local copies, waits for them, and re-layouts  43.7 us (9%)
  other arithmetic  23.2 us (5%)
  between operations  14.6 us (3%)
  matrix products  10.1 us (2%)
    unnamed x2, waiting for transfers between devices  268 us
    all_to_all x1, blocking collectives, side_by_side(): lax.all_to_all(both, axis, split_axis=split_dim, concat_axis=concat_dim,...  65 us
    ppermute x6, starting transfers between devices, shifted(): return lax.ppermute(shard, axis, pairs)  19.6 us
    all_to_all x1, starting transfers between devices, project_keys(): lax.all_to_all(jnp.stack([key_weight] * lax.axis_size(('dp', 'seq'))), ('...  13.8 us
    reduce_sum x1, other arithmetic, block_targets(): table = jnp.sum(jnp.where(matches, label_prob[..., None], 0.0), axis=2)  13.3 us
    all_to_all x1, starting transfers between devices, move_rows(): lax.all_to_all(row_places, 'seq', split_axis=0, concat_axis=0, tiled=True)  13.2 us
    all_to_all x1, waiting for transfers between devices, project_keys(): lax.all_to_all(jnp.stack([key_weight] * lax.axis_size(('dp', 'seq'))), ('...  11.9 us
  transfers between devices with their start and end apart: 9, of which 7 were waited for; matrix products, arithmetic and copies ran while one was open for 11% of the time, Pallas kernels for 0%

profile of v1, /device:TPU:24, one launch (start us, length us, event | category | flops | bytes accessed | tf_op | source)
XLA Modules:
  0.0 495.1 jit_solution(15089956168966462097)
XLA Ops:
  10.0 13.2 %all-to-all-start = ((s32[32,6,1]{1,2,0:T(1,128)}), s32[32,6,1]{1,2,0:T(1,128)S(1)}, u32[]{:S(2)}, u32[]{:S(2)}) async-start(s32[32,6,1]{1,2,0:T(1,128)} %bitcast), calls=%async_computation | async-start | bytes 32768 | tf_op jit(solution)/shard_map/all_to_all | solution.py:80
  23.2 1.5 scatter_custom_fusion.3
  24.6 2.1 scatter_custom_fusion.2
  26.8 2.1 scatter_custom_fusion.1
  29.0 1.7 all_to_all.22
  30.7 2.1 all-to-all-done
  32.8 65.0 %all_to_all.29 = bf16[32,6,4608]{2,1,0:T(8,128)(2,1)S(1)} all-to-all(bf16[32,6,4608]{2,1,0:T(8,128)(2,1)} %all_to_all.22), channel_id=1, replica_groups=mesh['dp'=16,'seq'=32] {'seq'}, dimensions={0} | all-to-all | bytes 3538944 | tf_op jit(solution)/shard_map/all_to_all | solution.py:20
  97.8 1.8 stack.18
  99.7 13.8 %all-to-all-start.2 = ((bf16[512,4,512]{2,1,0:T(4,128)(2,1)}), bf16[512,4,512]{2,1,0:T(4,128)(2,1)}, u32[]{:S(2)}, u32[]{:S(2)}) async-start(bf16[512,4,512]{2,1,0:T(4,128)(2,1)} %stack.18), calls=%async_computation.2 | async-start | bytes 4194304 | tf_op jit(solution)/shard_map/all_to_all | solution.py:68
  117.6 2.2 copy.100
  119.8 2.2 copy.102
  123.4 13.3 %select_reduce_fusion.1 = (f32[128,16,128]{2,1,0:T(8,128)}, f32[128,16,128]{2,1,0:T(8,128)}, f32[128,16,128]{2,1,0:T(8,128)}) fusion(s32[128,16,8]{2,1,0:T(8,128)} %copy.100, f32[128,16,8]{2,1,0:T(8,128)} %copy.98, s32[128,16,8]{2,1,0:T(8,128)} %copy.102, s32[128,16,8]{2,1,0:T(8,128)S(1)} %copy.96), kind=kLoop, calls=%fused_computation.9 | loop fusion | flops 18087936 | bytes 3407872 | tf_op jit(solution)/shard_map/reduce_sum | solution.py:60
  136.8 2.7 copy.101
  139.5 2.6 copy.103
  142.0 1.4 copy.99
  145.0 1.4 reduce.12
  146.5 1.6 all_to_all.24
  148.1 2.4 scatter_custom_fusion.5
  150.6 2.4 scatter_custom_fusion.6
  153.3 11.9 %all-to-all-done.2 = bf16[512,4,512]{2,1,0:T(4,128)(2,1)} async-done(((bf16[512,4,512]{2,1,0:T(4,128)(2,1)}), bf16[512,4,512]{2,1,0:T(4,128)(2,1)}, u32[]{:S(2)}, u32[]{:S(2)}) %all-to-all-start.2) | async-done | bytes 2097184 | tf_op jit(solution)/shard_map/all_to_all | solution.py:68
  165.2 2.5 reshape.459
  167.8 2.5 copy.81
  170.3 2.4 fusion.20
  172.7 2.2 collective-permute-start.1
  174.9 3.7 collective-permute-start
  187.7 4.2 collective-permute-done.4
  191.9 4.1 collective-permute-done.5
  196.1 2.7 convolution_multiply_fusion
  198.8 1.8 scatter_custom_fusion.4
  200.6 7.3 %collective-permute-start.3 = (bf16[128,512]{1,0:T(8,128)(2,1)S(1)}, bf16[128,512]{1,0:T(8,128)(2,1)}, u32[]{:S(2)}, u32[]{:S(2)}) collective-permute-start(bf16[128,512]{1,0:T(8,128)(2,1)S(1)} %scatter_custom_fusion.4), channel_id=1, source_target_pairs={{0,2},{1,3},{2,4},{3,5},{4,6},{5,7},{6,8},{7,9},{8,10},{9,11},{10,... | collective-permute-start | bytes 393224 | tf_op jit(solution)/shard_map/ppermute | solution.py:30
  207.8 3.9 collective-permute-start.2
  218.7 268.2 %all-reduce.3.cloned.1.call-done = f32[2048,512]{1,0:T(8,128)} async-done(((f32[2048,512]{1,0:T(8,128)}), f32[2048,512]{1,0:T(8,128)}) %all-reduce.3.cloned.1.call-update) | async-done | bytes 4194320
  (103 shorter events, 27.4 us)
Async XLA Ops:
  10.0 22.9 %all-to-all-start = ((s32[32,6,1]{1,2,0:T(1,128)}), s32[32,6,1]{1,2,0:T(1,128)S(1)}, u32[]{:S(2)}, u32[]{:S(2)}) async-start(s32[32,6,1]{1,2,0:T(1,128)} %bitcast), calls=%async_computation | async-start | bytes 32768 | tf_op jit(solution)/shard_map/all_to_all | solution.py:80
  30.7 67.1 %copy-start.16 = (bf16[4,512]{1,0:T(4,128)(2,1)S(1)}, bf16[4,512]{1,0:T(4,128)(2,1)}, u32[]{:S(2)}) copy-start(bf16[4,512]{1,0:T(4,128)(2,1)} %param.12) | copy-start | bytes 12292
  32.8 66.8 %copy-start.12 = (s32[32,6,1]{1,2,0:T(1,128)}, s32[32,6,1]{1,2,0:T(1,128)S(1)}, u32[]{:S(2)}) copy-start(s32[32,6,1]{1,2,0:T(1,128)S(1)} %all-to-all-done) | copy-start | bytes 2308
  99.7 14.1 %copy-start.17 = (s32[1,64]{1,0:T(1,128)S(1)}, s32[1,64]{1,0:T(1,128)}, u32[]{:S(2)}) copy-start(s32[1,64]{1,0:T(1,128)} %param.13) | copy-start | bytes 772
  99.7 14.4 %copy-start.10 = (f32[128,128]{1,0:T(8,128)S(1)}, f32[128,128]{1,0:T(8,128)}, u32[]{:S(2)}) copy-start(f32[128,128]{1,0:T(8,128)} %param.15) | copy-start | bytes 196612
  99.7 14.5 %copy-start.11 = (s32[128,128]{1,0:T(8,128)S(1)}, s32[128,128]{1,0:T(8,128)}, u32[]{:S(2)}) copy-start(s32[128,128]{1,0:T(8,128)} %param.14) | copy-start | bytes 196612
  99.7 65.5 %all-to-all-start.2 = ((bf16[512,4,512]{2,1,0:T(4,128)(2,1)}), bf16[512,4,512]{2,1,0:T(4,128)(2,1)}, u32[]{:S(2)}, u32[]{:S(2)}) async-start(bf16[512,4,512]{2,1,0:T(4,128)(2,1)} %stack.18), calls=%async_computation.2 | async-start | bytes 4194304 | tf_op jit(solution)/shard_map/all_to_all | solution.py:68
  113.5 373.4 %all-reduce.3.cloned.1.call-start = ((), (), s32[]{:S(2)}) async-start(), calls=%async_computation.3 | async-start | bytes 8388608
  136.8 5.2 %copy-start.5 = (f32[128,16,128]{2,1,0:T(8,128)S(1)}, f32[128,16,128]{2,1,0:T(8,128)}, u32[]{:S(2)}) copy-start(f32[128,16,128]{2,1,0:T(8,128)} %get-tuple-element.19) | copy-start | bytes 3145732
  143.6 39.9 %copy-start.8 = (pred[128,128]{0,1:T(8,128)(4,1)}, pred[128,128]{0,1:T(8,128)(4,1)S(1)}, u32[]{:S(2)}) copy-start(pred[128,128]{0,1:T(8,128)(4,1)S(1)} %get-tuple-element.38) | copy-start | bytes 49156
  143.6 40.4 %copy-start.6 = (pred[128,128]{0,1:T(8,128)(4,1)}, pred[128,128]{0,1:T(8,128)(4,1)S(1)}, u32[]{:S(2)}) copy-start(pred[128,128]{0,1:T(8,128)(4,1)S(1)} %get-tuple-element.39) | copy-start | bytes 49156
  143.6 43.5 %copy-start.9 = (pred[128,128]{0,1:T(8,128)(4,1)}, pred[128,128]{0,1:T(8,128)(4,1)S(1)}, u32[]{:S(2)}) copy-start(pred[128,128]{0,1:T(8,128)(4,1)S(1)} %get-tuple-element.40) | copy-start | bytes 49156
  170.3 8.8 %copy-start.4 = (f32[16,128,128]{1,2,0:T(8,128)S(1)}, f32[16,128,128]{1,2,0:T(8,128)}, u32[]{:S(2)}) copy-start(f32[16,128,128]{1,2,0:T(8,128)} %copy.99) | copy-start | bytes 3145732
  172.7 8.6 %collective-permute-start.1 = (bf16[128,512]{0,1:T(8,128)(2,1)S(1)}, bf16[128,512]{0,1:T(8,128)(2,1)S(1)}, u32[]{:S(2)}, u32[]{:S(2)}) collective-permute-start(bf16[128,512]{0,1:T(8,128)(2,1)S(1)} %bitcast.183), channel_id=1, source_target_pairs={{0,2},{1,3},{2,4},{3,5},{4,6},{5,7},{6,8},{7,9},{8,10},{9,11},{10,... | collective-permute-start | bytes 393224 | tf_op jit(solution)/shard_map/ppermute | solution.py:30
  174.9 6.0 %collective-permute-start = (bf16[128,512]{0,1:T(8,128)(2,1)S(1)}, bf16[128,512]{0,1:T(8,128)(2,1)S(1)}, u32[]{:S(2)}, u32[]{:S(2)}) collective-permute-start(bf16[128,512]{0,1:T(8,128)(2,1)S(1)} %bitcast.184), channel_id=1, source_target_pairs={{0,1},{1,2},{2,3},{3,4},{4,5},{5,6},{6,7},{7,8},{8,9},{9,10},{10,1... | collective-permute-start | bytes 393224 | tf_op jit(solution)/shard_map/ppermute | solution.py:30
  179.1 8.1 %copy-start = (f32[4,4,128,128]{2,3,1,0:T(8,128)}, f32[4,4,128,128]{2,3,1,0:T(8,128)S(1)}, u32[]{:S(2)}) copy-start(f32[4,4,128,128]{2,3,1,0:T(8,128)S(1)} %get-tuple-element.44) | copy-start | bytes 3145732
  179.1 2.7 copy-start.2
  181.3 1.3 copy-start.3
  184.6 7.3 %collective-permute-start.4 = (bf16[128,512]{0,1:T(8,128)(2,1)S(1)}, bf16[128,512]{0,1:T(8,128)(2,1)S(1)}, u32[]{:S(2)}, u32[]{:S(2)}) collective-permute-start(bf16[128,512]{0,1:T(8,128)(2,1)S(1)} %bitcast.182), channel_id=1, source_target_pairs={{1,0},{2,1},{3,2},{4,3},{5,4},{6,5},{7,6},{8,7},{9,8},{10,9},{11,1... | collective-permute-start | bytes 393224 | tf_op jit(solution)/shard_map/ppermute | solution.py:30
  185.9 10.1 %collective-permute-start.5 = (bf16[128,512]{0,1:T(8,128)(2,1)S(1)}, bf16[128,512]{0,1:T(8,128)(2,1)S(1)}, u32[]{:S(2)}, u32[]{:S(2)}) collective-permute-start(bf16[128,512]{0,1:T(8,128)(2,1)S(1)} %bitcast.181), channel_id=1, source_target_pairs={{2,0},{3,1},{4,2},{5,3},{6,4},{7,5},{8,6},{9,7},{10,8},{11,9},{12,... | collective-permute-start | bytes 393224 | tf_op jit(solution)/shard_map/ppermute | solution.py:30
  198.8 15.8 %copy-start.1 = (f32[4,4,128,128]{2,3,1,0:T(8,128)S(1)}, f32[4,4,128,128]{2,3,1,0:T(8,128)}, u32[]{:S(2)}) copy-start(f32[4,4,128,128]{2,3,1,0:T(8,128)} %copy-done) | copy-start | bytes 3145732
  200.6 11.9 %collective-permute-start.3 = (bf16[128,512]{1,0:T(8,128)(2,1)S(1)}, bf16[128,512]{1,0:T(8,128)(2,1)}, u32[]{:S(2)}, u32[]{:S(2)}) collective-permute-start(bf16[128,512]{1,0:T(8,128)(2,1)S(1)} %scatter_custom_fusion.4), channel_id=1, source_target_pairs={{0,2},{1,3},{2,4},{3,5},{4,6},{5,7},{6,8},{7,9},{8,10},{9,11},{10,... | collective-permute-start | bytes 393224 | tf_op jit(solution)/shard_map/ppermute | solution.py:30
  207.8 5.7 %collective-permute-start.2 = (bf16[128,512]{1,0:T(8,128)(2,1)S(1)}, bf16[128,512]{1,0:T(8,128)(2,1)}, u32[]{:S(2)}, u32[]{:S(2)}) collective-permute-start(bf16[128,512]{1,0:T(8,128)(2,1)S(1)} %scatter_custom_fusion.4), channel_id=1, source_target_pairs={{0,1},{1,2},{2,3},{3,4},{4,5},{5,6},{6,7},{7,8},{8,9},{9,10},{10,1... | collective-permute-start | bytes 393224 | tf_op jit(solution)/shard_map/ppermute | solution.py:30
  214.6 2.2 copy-start.7
  216.7 1.4 copy-start.13
  216.7 1.4 copy-start.14
  216.7 1.4 copy-start.15
  216.8 1.5 copy-start.18
Sparse Core Ops, SparseCore 0:
  198.9 287.9 all-reduce.2
